TPU v7x, 512 devices: a whole 4x8x8 slice. The times are simulated.
512 devices in a mesh: row: 32 (over z, x_lo, core), col: 16 (over x_hi, y).
Axes of the slice: x: 4 (x_hi: 2, x_lo: 2; x = x_hi * 2 + x_lo), y: 8, z: 8, core: 2. Of those that a mesh axis runs over, the one named last changes fastest.
Arguments:
- slab_block: bfloat16 [65536, 2048], P('row', 'col'), may hold values from -6 to 6
- scale_first: bfloat16 [65536], P('row'), may hold values from 0.5 to 2
- scale_second: bfloat16 [65536], P('row'), may hold values from 0.5 to 2
- panel_lower: bfloat16 [65536, 4096], P('row', 'col'), may hold values from -0.09375 to 0.09375
Outputs:
- updated_slab: bfloat16 [65536, 2048], P('row', 'col')
All inputs are finite; a program needn't handle non-finite values.
Results may differ from a plain program's by a relative error of at most 0.015.
Values may be sent and summed in bfloat16 or wider, within the bound.
No kernel may reach another device: no remote copies, remote signals or barrier semaphores. Data moves between devices by JAX's collectives and lax.ppermute only.
A program may use at most 64 MiB of HBM per device.

v0:
```python
import jax
import jax.numpy as jnp
from jax import lax
from jax.sharding import Mesh, PartitionSpec as P

PANEL_W = 4096
X_HI = 2
CHUNKS = 4
inv_root = 0.7071067811865476


def butterfly(top, bottom):
    top = top.astype(jnp.float32)
    bottom = bottom.astype(jnp.float32)
    return jnp.concatenate([(top + bottom) * inv_root, (top - bottom) * inv_root], axis=0)


def per_device(slab_block, scale_first, scale_second, panel_lower):
    row_count, col_width = slab_block.shape
    groups = lax.axis_size("row")
    y_count = lax.axis_size("y")
    block_width = panel_lower.shape[1]
    chunk = row_count // CHUNKS
    gathered = [
        lax.all_gather(panel_lower[c * chunk : (c + 1) * chunk], "y", axis=1, tiled=True)
        for c in range(CHUNKS)
    ]
    first = (scale_first.astype(jnp.float32)[:, None] * slab_block.astype(jnp.float32)).astype(
        jnp.bfloat16
    )
    cyclic = lax.all_to_all(
        first.reshape(row_count // groups, groups, col_width),
        "row",
        split_axis=1,
        concat_axis=0,
        tiled=True,
    ).reshape(row_count, col_width)
    scale_cyclic = lax.all_to_all(
        scale_second.reshape(row_count // groups, groups),
        "row",
        split_axis=1,
        concat_axis=0,
        tiled=True,
    ).reshape(row_count)
    half = row_count // 2
    quarter = row_count // 4
    level_one = butterfly(cyclic[:half], cyclic[half:])
    second = (scale_cyclic.astype(jnp.float32)[:, None] * level_one).astype(jnp.bfloat16)
    stored = jnp.concatenate(
        [
            butterfly(second[:quarter], second[quarter:half]),
            butterfly(second[half : half + quarter], second[half + quarter :]),
        ],
        axis=0,
    ).astype(jnp.bfloat16)
    top_count = PANEL_W // groups // X_HI
    top = stored[: top_count * X_HI].reshape(1, X_HI, top_count, col_width)
    send = jnp.broadcast_to(top, (groups, X_HI, top_count, col_width)).reshape(
        groups * X_HI, top_count, col_width
    )
    got = lax.all_to_all(send, ("row", "x_hi"), split_axis=0, concat_axis=0)
    got = got.reshape(groups, X_HI, top_count, col_width)
    upper = jnp.transpose(got, (1, 2, 0, 3)).reshape(X_HI, top_count * groups, col_width)
    mine = lax.axis_index("x_hi")
    upper_own = lax.dynamic_index_in_dim(upper, mine, 0, keepdims=False)
    upper_far = lax.dynamic_index_in_dim(upper, 1 - mine, 0, keepdims=False)
    swap = [(i, X_HI - 1 - i) for i in range(X_HI)]
    out = []
    for c in range(CHUNKS):
        far = jnp.dot(gathered[c], upper_far, preferred_element_type=jnp.float32).astype(
            jnp.bfloat16
        )
        came = lax.ppermute(far, "x_hi", swap)
        own = jnp.dot(gathered[c], upper_own, preferred_element_type=jnp.float32)
        base = stored[c * chunk : (c + 1) * chunk].astype(jnp.float32)
        out.append((base - (own + came.astype(jnp.float32))).astype(jnp.bfloat16))
    return jnp.concatenate(out, axis=0)


def solution(mesh):
    rows, cols = mesh.devices.shape
    split = Mesh(mesh.devices.reshape(rows, X_HI, cols // X_HI), ("row", "x_hi", "y"))
    col = ("x_hi", "y")
    placed = (P("row", col), P("row"), P("row"), P("row", col))
    return jax.shard_map(
        per_device, mesh=split, in_specs=placed, out_specs=P("row", col), check_vma=False
    )
```

profile of v0, /device:TPU:16, one launch (start us, length us, event | category | flops | bytes accessed | tf_op | source)
XLA Modules:
  0.0 237.5 jit_solution(13325261711682254845)
XLA Ops:
  6.5 2.3 fusion.47
  8.8 0.0 all-gather.5.cloned.1.call-update
  8.9 0.0 all-gather.7.cloned.1.call-start
  8.9 0.7 all-gather.7.cloned.1.call-update
  9.6 0.0 all-gather.9.cloned.1.call-start
  9.7 0.7 all-gather.9.cloned.1.call-update
  10.4 0.1 all_to_all.24
  10.4 0.7 copy.21
  11.1 11.6 %all-to-all-start = ((bf16[64,32,1]{0,2,1:T(2,128)(2,1)}), bf16[64,32,1]{0,2,1:T(2,128)(2,1)S(1)}, u32[]{:S(2)}, u32[]{:S(2)}) async-start(bf16[64,32,1]{0,2,1:T(2,128)(2,1)} %copy.21), calls=%async_computation | async-start | bytes 32768 | tf_op jit(solution)/shard_map/all_to_all | solution.py:38
  22.8 0.3 multiply_convert_fusion
  23.1 1.0 copy.22
  24.1 6.9 %all-to-all-done = bf16[64,32,1]{0,2,1:T(2,128)(2,1)S(1)} async-done(((bf16[64,32,1]{0,2,1:T(2,128)(2,1)}), bf16[64,32,1]{0,2,1:T(2,128)(2,1)S(1)}, u32[]{:S(2)}, u32[]{:S(2)}) %all-to-all-start) | async-done | bytes 4128 | tf_op jit(solution)/shard_map/all_to_all | solution.py:38
  31.0 3.9 %all-to-all-start.1 = ((bf16[64,32,128]{2,0,1:T(8,128)(2,1)}), bf16[64,32,128]{2,0,1:T(8,128)(2,1)S(1)}, u32[]{:S(2)}, u32[]{:S(2)}) async-start(bf16[64,32,128]{2,0,1:T(8,128)(2,1)} %copy.22), calls=%async_computation.1 | async-start | bytes 1048576 | tf_op jit(solution)/shard_map/all_to_all | solution.py:31
  34.9 0.0 all-gather.11.cloned.1.call-start
  34.9 0.5 all-gather.11.cloned.1.call-update
  35.5 0.1 bitcast_reduce_fusion
  35.5 0.1 reshape.45
  35.6 17.3 %all-to-all-done.1 = bf16[64,32,128]{2,0,1:T(8,128)(2,1)S(1)} async-done(((bf16[64,32,128]{2,0,1:T(8,128)(2,1)}), bf16[64,32,128]{2,0,1:T(8,128)(2,1)S(1)}, u32[]{:S(2)}, u32[]{:S(2)}) %all-to-all-start.1) | async-done | bytes 524320 | tf_op jit(solution)/shard_map/all_to_all | solution.py:31
  52.9 0.1 fusion.5
  53.1 0.2 copy.23
  53.3 0.2 copy.24
  53.5 0.1 fusion.4
  53.5 0.0 copy-start.4
  53.6 0.8 copy-done.4
  54.4 0.1 copy.25
  54.5 1.3 broadcast_in_dim.10
  55.8 5.6 %all-to-all-start.2 = ((bf16[64,64,128]{2,1,0:T(8,128)(2,1)}), bf16[64,64,128]{2,1,0:T(8,128)(2,1)S(1)}, u32[]{:S(2)}, u32[]{:S(2)}) async-start(bf16[64,64,128]{2,1,0:T(8,128)(2,1)} %bitcast.8), calls=%async_computation.2 | async-start | bytes 2097152 | tf_op jit(solution)/shard_map/all_to_all | solution.py:61
  61.5 30.1 %all-to-all-done.2 = bf16[64,64,128]{2,1,0:T(8,128)(2,1)S(1)} async-done(((bf16[64,64,128]{2,1,0:T(8,128)(2,1)}), bf16[64,64,128]{2,1,0:T(8,128)(2,1)S(1)}, u32[]{:S(2)}, u32[]{:S(2)}) %all-to-all-start.2) | async-done | bytes 1048608 | tf_op jit(solution)/shard_map/all_to_all | solution.py:61
  91.6 0.7 copy.26
  92.3 0.0 all-gather.5.cloned.1.call-done
  92.3 3.1 %fusion = bf16[512,128]{0,1:T(8,128)(2,1)} fusion(bf16[512,2048]{1,0:T(8,128)(2,1)} %all-gather.5.cloned.1.call-done, bf16[2,2048,128]{2,1,0:T(8,128)(2,1)S(1)} %bitcast.72, s32[]{:T(128)S(6)} %select_n.8), kind=kOutput, calls=%fused_computation.8 | convolution fusion | flops 268500992 | bytes 2752516 | tf_op jit(solution)/shard_map/dot_general | solution.py:70
  95.4 3.7 %collective-permute-start = (bf16[512,128]{0,1:T(8,128)(2,1)}, bf16[512,128]{0,1:T(8,128)(2,1)S(1)}, u32[]{:S(2)}, u32[]{:S(2)}) collective-permute-start(bf16[512,128]{0,1:T(8,128)(2,1)} %fusion), channel_id=1, source_target_pairs={{0,8},{8,0},{1,9},{9,1},{2,10},{10,2},{3,11},{11,3},{4,12},{12,4},... | collective-permute-start | bytes 393224 | tf_op jit(solution)/shard_map/ppermute | solution.py:73
  99.1 16.7 %all-gather.7.cloned.1.call-done = bf16[512,2048]{1,0:T(8,128)(2,1)} async-done(((bf16[512,256]{1,0:T(8,128)(2,1)}), bf16[512,2048]{1,0:T(8,128)(2,1)}) %all-gather.7.cloned.1.call-update) | async-done | bytes 2097168 | tf_op jit(solution)/shard_map/all_gather | solution.py:25
  115.8 3.1 %fusion.1 = bf16[512,128]{0,1:T(8,128)(2,1)} fusion(bf16[512,2048]{1,0:T(8,128)(2,1)} %all-gather.7.cloned.1.call-done, bf16[2,2048,128]{2,1,0:T(8,128)(2,1)S(1)} %bitcast.73, s32[]{:T(128)S(6)} %select_n.8), kind=kOutput, calls=%fused_computation.9 | convolution fusion | flops 268500992 | bytes 2752516 | tf_op jit(solution)/shard_map/dot_general | solution.py:70
  118.8 3.0 %collective-permute-start.1 = (bf16[512,128]{0,1:T(8,128)(2,1)}, bf16[512,128]{0,1:T(8,128)(2,1)S(1)}, u32[]{:S(2)}, u32[]{:S(2)}) collective-permute-start(bf16[512,128]{0,1:T(8,128)(2,1)} %fusion.1), channel_id=1, source_target_pairs={{0,8},{8,0},{1,9},{9,1},{2,10},{10,2},{3,11},{11,3},{4,12},{12,4},... | collective-permute-start | bytes 393224 | tf_op jit(solution)/shard_map/ppermute | solution.py:73
  121.8 45.2 %all-gather.9.cloned.1.call-done = bf16[512,2048]{1,0:T(8,128)(2,1)} async-done(((bf16[512,256]{1,0:T(8,128)(2,1)}), bf16[512,2048]{1,0:T(8,128)(2,1)}) %all-gather.9.cloned.1.call-update) | async-done | bytes 2097168 | tf_op jit(solution)/shard_map/all_gather | solution.py:25
  167.0 3.1 %fusion.2 = bf16[512,128]{0,1:T(8,128)(2,1)} fusion(bf16[512,2048]{1,0:T(8,128)(2,1)} %all-gather.9.cloned.1.call-done, bf16[2,2048,128]{2,1,0:T(8,128)(2,1)S(1)} %bitcast.74, s32[]{:T(128)S(6)} %select_n.8), kind=kOutput, calls=%fused_computation.10 | convolution fusion | flops 268500992 | bytes 2752516 | tf_op jit(solution)/shard_map/dot_general | solution.py:70
  170.1 2.8 %collective-permute-start.2 = (bf16[512,128]{0,1:T(8,128)(2,1)}, bf16[512,128]{0,1:T(8,128)(2,1)}, u32[]{:S(2)}, u32[]{:S(2)}) collective-permute-start(bf16[512,128]{0,1:T(8,128)(2,1)} %fusion.2), channel_id=1, source_target_pairs={{0,8},{8,0},{1,9},{9,1},{2,10},{10,2},{3,11},{11,3},{4,12},{12,4},... | collective-permute-start | bytes 393224 | tf_op jit(solution)/shard_map/ppermute | solution.py:73
  172.9 45.2 %all-gather.11.cloned.1.call-done = bf16[512,2048]{1,0:T(8,128)(2,1)} async-done(((bf16[512,256]{1,0:T(8,128)(2,1)}), bf16[512,2048]{1,0:T(8,128)(2,1)}) %all-gather.11.cloned.1.call-update) | async-done | bytes 2097168 | tf_op jit(solution)/shard_map/all_gather | solution.py:25
  218.1 2.4 %fusion.3 = bf16[512,128]{0,1:T(8,128)(2,1)S(1)} fusion(bf16[512,2048]{1,0:T(8,128)(2,1)} %all-gather.11.cloned.1.call-done, bf16[2,2048,128]{2,1,0:T(8,128)(2,1)S(1)} %bitcast.75, s32[]{:T(128)S(6)} %select_n.8), kind=kOutput, calls=%fused_computation.11 | convolution fusion | flops 268500992 | bytes 2752516 | tf_op jit(solution)/shard_map/dot_general | solution.py:70
  220.5 2.9 %collective-permute-start.3 = (bf16[512,128]{0,1:T(8,128)(2,1)S(1)}, bf16[512,128]{0,1:T(8,128)(2,1)S(1)}, u32[]{:S(2)}, u32[]{:S(2)}) collective-permute-start(bf16[512,128]{0,1:T(8,128)(2,1)S(1)} %fusion.3), channel_id=1, source_target_pairs={{0,8},{8,0},{1,9},{9,1},{2,10},{10,2},{3,11},{11,3},{4,12},{12,4},... | collective-permute-start | bytes 393224 | tf_op jit(solution)/shard_map/ppermute | solution.py:73
  223.5 0.8 subtract_convert_fusion.3
  224.4 0.8 subtract_convert_fusion.2
  225.2 0.7 copy-done.2
  225.9 1.8 subtract_convert_fusion.1
  227.7 1.4 collective-permute-done.3
  229.0 0.9 subtract_convert_fusion
  230.0 1.0 copy.27
  (23 shorter events, 0.1 us)
Async XLA Ops:
  6.5 3.8 %copy-start.7 = (bf16[2048]{0:T(1024)(128)(2,1)S(1)}, bf16[2048]{0:T(1024)(128)(2,1)}, u32[]{:S(2)}) copy-start(bf16[2048]{0:T(1024)(128)(2,1)} %param.6) | copy-start | bytes 12292
  6.5 16.2 %copy-start.8 = (bf16[2048]{0:T(1024)(128)(2,1)S(1)}, bf16[2048]{0:T(1024)(128)(2,1)}, u32[]{:S(2)}) copy-start(bf16[2048]{0:T(1024)(128)(2,1)} %param.5) | copy-start | bytes 12292
  6.5 16.3 %copy-start.6 = (bf16[2048,128]{1,0:T(8,128)(2,1)S(1)}, bf16[2048,128]{1,0:T(8,128)(2,1)}, u32[]{:S(2)}) copy-start(bf16[2048,128]{1,0:T(8,128)(2,1)} %param.4) | copy-start | bytes 1572868
  6.5 85.8 %all-gather.5.cloned.1.call-start = ((), (), s32[]{:S(2)}) async-start(), calls=%async_computation.3 | async-start | bytes 2359296 | tf_op jit(solution)/shard_map/all_gather | solution.py:25
  8.9 106.9 %all-gather.7.cloned.1.call-start = ((), (), s32[]{:S(2)}) async-start(), calls=%async_computation.4 | async-start | bytes 2359296 | tf_op jit(solution)/shard_map/all_gather | solution.py:25
  9.6 157.4 %all-gather.9.cloned.1.call-start = ((), (), s32[]{:S(2)}) async-start(), calls=%async_computation.5 | async-start | bytes 2359296 | tf_op jit(solution)/shard_map/all_gather | solution.py:25
  11.1 19.9 %all-to-all-start = ((bf16[64,32,1]{0,2,1:T(2,128)(2,1)}), bf16[64,32,1]{0,2,1:T(2,128)(2,1)S(1)}, u32[]{:S(2)}, u32[]{:S(2)}) async-start(bf16[64,32,1]{0,2,1:T(2,128)(2,1)} %copy.21), calls=%async_computation | async-start | bytes 32768 | tf_op jit(solution)/shard_map/all_to_all | solution.py:38
  31.0 21.9 %all-to-all-start.1 = ((bf16[64,32,128]{2,0,1:T(8,128)(2,1)}), bf16[64,32,128]{2,0,1:T(8,128)(2,1)S(1)}, u32[]{:S(2)}, u32[]{:S(2)}) async-start(bf16[64,32,128]{2,0,1:T(8,128)(2,1)} %copy.22), calls=%async_computation.1 | async-start | bytes 1048576 | tf_op jit(solution)/shard_map/all_to_all | solution.py:31
  34.9 183.2 %all-gather.11.cloned.1.call-start = ((), (), s32[]{:S(2)}) async-start(), calls=%async_computation.6 | async-start | bytes 2359296 | tf_op jit(solution)/shard_map/all_gather | solution.py:25
  53.5 0.8 copy-start.4
  55.8 35.8 %all-to-all-start.2 = ((bf16[64,64,128]{2,1,0:T(8,128)(2,1)}), bf16[64,64,128]{2,1,0:T(8,128)(2,1)S(1)}, u32[]{:S(2)}, u32[]{:S(2)}) async-start(bf16[64,64,128]{2,1,0:T(8,128)(2,1)} %bitcast.8), calls=%async_computation.2 | async-start | bytes 2097152 | tf_op jit(solution)/shard_map/all_to_all | solution.py:61
  95.4 128.1 %collective-permute-start = (bf16[512,128]{0,1:T(8,128)(2,1)}, bf16[512,128]{0,1:T(8,128)(2,1)S(1)}, u32[]{:S(2)}, u32[]{:S(2)}) collective-permute-start(bf16[512,128]{0,1:T(8,128)(2,1)} %fusion), channel_id=1, source_target_pairs={{0,8},{8,0},{1,9},{9,1},{2,10},{10,2},{3,11},{11,3},{4,12},{12,4},... | collective-permute-start | bytes 393224 | tf_op jit(solution)/shard_map/ppermute | solution.py:73
  118.8 104.6 %copy-start = (bf16[512,2048]{1,0:T(8,128)(2,1)S(1)}, bf16[512,2048]{1,0:T(8,128)(2,1)}, u32[]{:S(2)}) copy-start(bf16[512,2048]{1,0:T(8,128)(2,1)} %all-gather.5.cloned.1.call-done) | copy-start | bytes 6291460
  118.8 105.5 %collective-permute-start.1 = (bf16[512,128]{0,1:T(8,128)(2,1)}, bf16[512,128]{0,1:T(8,128)(2,1)S(1)}, u32[]{:S(2)}, u32[]{:S(2)}) collective-permute-start(bf16[512,128]{0,1:T(8,128)(2,1)} %fusion.1), channel_id=1, source_target_pairs={{0,8},{8,0},{1,9},{9,1},{2,10},{10,2},{3,11},{11,3},{4,12},{12,4},... | collective-permute-start | bytes 393224 | tf_op jit(solution)/shard_map/ppermute | solution.py:73
  170.1 55.1 %collective-permute-start.2 = (bf16[512,128]{0,1:T(8,128)(2,1)}, bf16[512,128]{0,1:T(8,128)(2,1)}, u32[]{:S(2)}, u32[]{:S(2)}) collective-permute-start(bf16[512,128]{0,1:T(8,128)(2,1)} %fusion.2), channel_id=1, source_target_pairs={{0,8},{8,0},{1,9},{9,1},{2,10},{10,2},{3,11},{11,3},{4,12},{12,4},... | collective-permute-start | bytes 393224 | tf_op jit(solution)/shard_map/ppermute | solution.py:73
  220.5 3.8 %copy-start.1 = (bf16[512,2048]{1,0:T(8,128)(2,1)S(1)}, bf16[512,2048]{1,0:T(8,128)(2,1)}, u32[]{:S(2)}) copy-start(bf16[512,2048]{1,0:T(8,128)(2,1)} %all-gather.7.cloned.1.call-done) | copy-start | bytes 6291460
  220.5 3.8 %copy-start.5 = (bf16[2048,128]{0,1:T(8,128)(2,1)S(1)}, bf16[2048,128]{0,1:T(8,128)(2,1)}, u32[]{:S(2)}) copy-start(bf16[2048,128]{0,1:T(8,128)(2,1)} %copy-done.4) | copy-start | bytes 1572868
  220.5 8.5 %collective-permute-start.3 = (bf16[512,128]{0,1:T(8,128)(2,1)S(1)}, bf16[512,128]{0,1:T(8,128)(2,1)S(1)}, u32[]{:S(2)}, u32[]{:S(2)}) collective-permute-start(bf16[512,128]{0,1:T(8,128)(2,1)S(1)} %fusion.3), channel_id=1, source_target_pairs={{0,8},{8,0},{1,9},{9,1},{2,10},{10,2},{3,11},{11,3},{4,12},{12,4},... | collective-permute-start | bytes 393224 | tf_op jit(solution)/shard_map/ppermute | solution.py:73
  224.3 1.6 copy-start.2
  225.2 3.8 %copy-start.3 = (bf16[512,2048]{1,0:T(8,128)(2,1)S(1)}, bf16[512,2048]{1,0:T(8,128)(2,1)}, u32[]{:S(2)}) copy-start(bf16[512,2048]{1,0:T(8,128)(2,1)} %all-gather.11.cloned.1.call-done) | copy-start | bytes 6291460
Sparse Core Ops, SparseCore 0:
  9.4 55.1 all-gather.4
  66.6 49.1 all-gather.6
  117.8 49.2 all-gather.8
  168.9 49.1 all-gather.10
where the time goes:
time: 238 us; the launch traced here: 237 us
  waiting for transfers between devices  165 us (69%)
  starting transfers between devices  33.6 us (14%)
  matrix products  15.9 us (7%)
  between operations  13.4 us (6%)
  local copies, waits for them, and re-layouts  9.13 us (4%)
    all_gather x4, waiting for transfers between devices, per_device(): lax.all_gather(panel_lower[c * chunk:(c + 1) * chunk], 'y', axis=1, tiled...  107 us
    all_to_all x1, waiting for transfers between devices, per_device(): got = lax.all_to_all(send, ('row', 'x_hi'), split_axis=0, concat_axis=0)  30.1 us
    all_to_all x1, waiting for transfers between devices, per_device(): lax.all_to_all(first.reshape(row_count // groups, groups, col_width), 'ro...  17.3 us
    ppermute x4, starting transfers between devices, per_device(): came = lax.ppermute(far, 'x_hi', swap)  12.3 us
    dot_general x4, matrix products, per_device(): jnp.dot(gathered[c], upper_far, preferred_element_type=jnp.float32)  11.7 us
    all_to_all x1, starting transfers between devices, per_device(): lax.all_to_all(scale_second.reshape(row_count // groups, groups), 'row',...  11.6 us
    all_to_all x1, waiting for transfers between devices, per_device(): lax.all_to_all(scale_second.reshape(row_count // groups, groups), 'row',...  6.85 us
    all_to_all x1, starting transfers between devices, per_device(): got = lax.all_to_all(send, ('row', 'x_hi'), split_axis=0, concat_axis=0)  5.65 us
  transfers between devices with their start and end apart: 11, of which 7 were waited for; matrix products, arithmetic and copies ran while one was open for 8% of the time, Pallas kernels for 0%

commit v1 on v0

--- a/solution.py
+++ b/solution.py
@@ -22,7 +22,15 @@
     block_width = panel_lower.shape[1]
     chunk = row_count // CHUNKS
     gathered = [
-        lax.all_gather(panel_lower[c * chunk : (c + 1) * chunk], "y", axis=1, tiled=True)
+        jnp.concatenate(
+            lax.all_to_all(
+                jnp.stack([panel_lower[c * chunk : (c + 1) * chunk]] * lax.axis_size("y")),
+                "y",
+                0,
+                0,
+            ),
+            axis=1,
+        )
         for c in range(CHUNKS)
     ]
     first = (scale_first.astype(jnp.float32)[:, None] * slab_block.astype(jnp.float32)).astype(

time: 238 us -> 323 us (1.36)
  the two profiles are of different devices: /device:TPU:16 before, /device:TPU:10 now
where the time goes in v1:
time: 323 us; the launch traced here: 322 us
  waiting for transfers between devices  227 us (70%)
  starting transfers between devices  60.5 us (19%)
  local copies, waits for them, and re-layouts  16.6 us (5%)
  matrix products  14.8 us (5%)
    all_to_all x4, waiting for transfers between devices, per_device(): lax.all_to_all(jnp.stack([panel_lower[c * chunk:(c + 1) * chunk]] * lax.a...  178 us
    all_to_all x1, waiting for transfers between devices, per_device(): got = lax.all_to_all(send, ('row', 'x_hi'), split_axis=0, concat_axis=0)  27.8 us
    all_to_all x4, starting transfers between devices, per_device(): lax.all_to_all(jnp.stack([panel_lower[c * chunk:(c + 1) * chunk]] * lax.a...  23.5 us
    all_to_all x1, waiting for transfers between devices, per_device(): lax.all_to_all(first.reshape(row_count // groups, groups, col_width), 'ro...  17.7 us
    ppermute x4, starting transfers between devices, per_device(): came = lax.ppermute(far, 'x_hi', swap)  14.6 us
    all_to_all x1, starting transfers between devices, per_device(): lax.all_to_all(scale_second.reshape(row_count // groups, groups), 'row',...  11.9 us
    dot_general x4, matrix products, per_device(): jnp.dot(gathered[c], upper_far, preferred_element_type=jnp.float32)  8.08 us
    dot_general x4, matrix products, per_device(): own = jnp.dot(gathered[c], upper_own, preferred_element_type=jnp.float32)  6.74 us
  transfers between devices with their start and end apart: 11, of which 7 were waited for; matrix products, arithmetic and copies ran while one was open for 6% of the time, Pallas kernels for 0%

profile of v1, /device:TPU:10, one launch (start us, length us, event | category | flops | bytes accessed | tf_op | source)
XLA Modules:
  0.0 322.0 jit_solution(11787050918068308856)
XLA Ops:
  0.0 0.8 all_to_all.36
  0.8 0.7 copy.29
  1.5 11.9 %all-to-all-start = ((bf16[64,32,1]{0,2,1:T(2,128)(2,1)}), bf16[64,32,1]{0,2,1:T(2,128)(2,1)S(1)}, u32[]{:S(2)}, u32[]{:S(2)}) async-start(bf16[64,32,1]{0,2,1:T(2,128)(2,1)} %copy.29), calls=%async_computation | async-start | bytes 32768 | tf_op jit(solution)/shard_map/all_to_all | solution.py:46
  13.4 0.7 convert_element_type.109
  14.1 1.4 multiply_convert_fusion
  15.5 1.0 copy.30
  16.5 4.1 %all-to-all-done = bf16[64,32,1]{0,2,1:T(2,128)(2,1)S(1)} async-done(((bf16[64,32,1]{0,2,1:T(2,128)(2,1)}), bf16[64,32,1]{0,2,1:T(2,128)(2,1)S(1)}, u32[]{:S(2)}, u32[]{:S(2)}) %all-to-all-start) | async-done | bytes 4128 | tf_op jit(solution)/shard_map/all_to_all | solution.py:46
  20.5 4.7 %all-to-all-start.1 = ((bf16[64,32,128]{2,0,1:T(8,128)(2,1)}), bf16[64,32,128]{2,0,1:T(8,128)(2,1)S(1)}, u32[]{:S(2)}, u32[]{:S(2)}) async-start(bf16[64,32,128]{2,0,1:T(8,128)(2,1)} %copy.30), calls=%async_computation.1 | async-start | bytes 1048576 | tf_op jit(solution)/shard_map/all_to_all | solution.py:39
  25.4 17.7 %all-to-all-done.1 = bf16[64,32,128]{2,0,1:T(8,128)(2,1)S(1)} async-done(((bf16[64,32,128]{2,0,1:T(8,128)(2,1)}), bf16[64,32,128]{2,0,1:T(8,128)(2,1)S(1)}, u32[]{:S(2)}, u32[]{:S(2)}) %all-to-all-start.1) | async-done | bytes 524320 | tf_op jit(solution)/shard_map/all_to_all | solution.py:39
  43.1 0.1 fusion.5
  43.2 0.2 copy.32
  43.4 0.2 copy.31
  43.7 0.8 copy-done.1
  44.5 0.1 copy.33
  44.7 1.3 broadcast_in_dim.10
  45.9 5.8 %all-to-all-start.2 = ((bf16[64,64,128]{2,1,0:T(8,128)(2,1)}), bf16[64,64,128]{2,1,0:T(8,128)(2,1)S(1)}, u32[]{:S(2)}, u32[]{:S(2)}) async-start(bf16[64,64,128]{2,1,0:T(8,128)(2,1)} %bitcast.8), calls=%async_computation.2 | async-start | bytes 2097152 | tf_op jit(solution)/shard_map/all_to_all | solution.py:69
  51.7 0.9 fusion.47
  52.6 0.1 copy.38
  52.8 27.8 %all-to-all-done.2 = bf16[64,64,128]{2,1,0:T(8,128)(2,1)S(1)} async-done(((bf16[64,64,128]{2,1,0:T(8,128)(2,1)}), bf16[64,64,128]{2,1,0:T(8,128)(2,1)S(1)}, u32[]{:S(2)}, u32[]{:S(2)}) %all-to-all-start.2) | async-done | bytes 1048608 | tf_op jit(solution)/shard_map/all_to_all | solution.py:69
  80.5 1.6 stack.11
  82.1 7.5 %all-to-all-start.6 = ((bf16[8,512,256]{1,2,0:T(8,128)(2,1)}), bf16[8,512,256]{1,2,0:T(8,128)(2,1)S(1)}, u32[]{:S(2)}, u32[]{:S(2)}) async-start(bf16[8,512,256]{1,2,0:T(8,128)(2,1)} %stack.11), calls=%async_computation.6 | async-start | bytes 4194304 | tf_op jit(solution)/shard_map/all_to_all | solution.py:26
  89.7 1.1 copy.37
  90.8 47.9 %all-to-all-done.6 = bf16[8,512,256]{1,2,0:T(8,128)(2,1)S(1)} async-done(((bf16[8,512,256]{1,2,0:T(8,128)(2,1)}), bf16[8,512,256]{1,2,0:T(8,128)(2,1)S(1)}, u32[]{:S(2)}, u32[]{:S(2)}) %all-to-all-start.6) | async-done | bytes 2097184 | tf_op jit(solution)/shard_map/all_to_all | solution.py:26
  138.6 1.5 stack.10
  140.1 5.9 %all-to-all-start.5 = ((bf16[8,512,256]{1,2,0:T(8,128)(2,1)}), bf16[8,512,256]{1,2,0:T(8,128)(2,1)}, u32[]{:S(2)}, u32[]{:S(2)}) async-start(bf16[8,512,256]{1,2,0:T(8,128)(2,1)} %stack.10), calls=%async_computation.5 | async-start | bytes 4194304 | tf_op jit(solution)/shard_map/all_to_all | solution.py:26
  146.0 0.1 copy.36
  146.2 49.8 %all-to-all-done.5 = bf16[8,512,256]{1,2,0:T(8,128)(2,1)} async-done(((bf16[8,512,256]{1,2,0:T(8,128)(2,1)}), bf16[8,512,256]{1,2,0:T(8,128)(2,1)}, u32[]{:S(2)}, u32[]{:S(2)}) %all-to-all-start.5) | async-done | bytes 2097184 | tf_op jit(solution)/shard_map/all_to_all | solution.py:26
  196.0 1.5 stack.9
  197.6 4.3 %all-to-all-start.4 = ((bf16[8,512,256]{1,2,0:T(8,128)(2,1)}), bf16[8,512,256]{1,2,0:T(8,128)(2,1)}, u32[]{:S(2)}, u32[]{:S(2)}) async-start(bf16[8,512,256]{1,2,0:T(8,128)(2,1)} %stack.9), calls=%async_computation.4 | async-start | bytes 4194304 | tf_op jit(solution)/shard_map/all_to_all | solution.py:26
  201.9 0.1 copy.35
  202.0 48.8 %all-to-all-done.4 = bf16[8,512,256]{1,2,0:T(8,128)(2,1)} async-done(((bf16[8,512,256]{1,2,0:T(8,128)(2,1)}), bf16[8,512,256]{1,2,0:T(8,128)(2,1)}, u32[]{:S(2)}, u32[]{:S(2)}) %all-to-all-start.4) | async-done | bytes 2097184 | tf_op jit(solution)/shard_map/all_to_all | solution.py:26
  250.8 1.5 stack.8
  252.3 5.7 %all-to-all-start.3 = ((bf16[8,512,256]{1,2,0:T(8,128)(2,1)}), bf16[8,512,256]{1,2,0:T(8,128)(2,1)}, u32[]{:S(2)}, u32[]{:S(2)}) async-start(bf16[8,512,256]{1,2,0:T(8,128)(2,1)} %stack.8), calls=%async_computation.3 | async-start | bytes 4194304 | tf_op jit(solution)/shard_map/all_to_all | solution.py:26
  258.0 1.9 copy.34
  259.9 0.5 fusion.3
  260.4 3.6 %collective-permute-start.3 = (bf16[512,128]{0,1:T(8,128)(2,1)S(1)}, bf16[512,128]{0,1:T(8,128)(2,1)S(1)}, u32[]{:S(2)}, u32[]{:S(2)}) collective-permute-start(bf16[512,128]{0,1:T(8,128)(2,1)S(1)} %fusion.3), channel_id=1, source_target_pairs={{0,8},{8,0},{1,9},{9,1},{2,10},{10,2},{3,11},{11,3},{4,12},{12,4},... | collective-permute-start | bytes 393224 | tf_op jit(solution)/shard_map/ppermute | solution.py:81
  264.1 2.7 fusion.2
  266.8 3.7 %collective-permute-start.2 = (bf16[512,128]{0,1:T(8,128)(2,1)}, bf16[512,128]{0,1:T(8,128)(2,1)}, u32[]{:S(2)}, u32[]{:S(2)}) collective-permute-start(bf16[512,128]{0,1:T(8,128)(2,1)} %fusion.2), channel_id=1, source_target_pairs={{0,8},{8,0},{1,9},{9,1},{2,10},{10,2},{3,11},{11,3},{4,12},{12,4},... | collective-permute-start | bytes 393224 | tf_op jit(solution)/shard_map/ppermute | solution.py:81
  270.5 2.7 fusion.1
  273.3 3.6 %collective-permute-start.1 = (bf16[512,128]{0,1:T(8,128)(2,1)}, bf16[512,128]{0,1:T(8,128)(2,1)}, u32[]{:S(2)}, u32[]{:S(2)}) collective-permute-start(bf16[512,128]{0,1:T(8,128)(2,1)} %fusion.1), channel_id=1, source_target_pairs={{0,8},{8,0},{1,9},{9,1},{2,10},{10,2},{3,11},{11,3},{4,12},{12,4},... | collective-permute-start | bytes 393224 | tf_op jit(solution)/shard_map/ppermute | solution.py:81
  276.9 31.5 %all-to-all-done.3 = bf16[8,512,256]{1,2,0:T(8,128)(2,1)} async-done(((bf16[8,512,256]{1,2,0:T(8,128)(2,1)}), bf16[8,512,256]{1,2,0:T(8,128)(2,1)}, u32[]{:S(2)}, u32[]{:S(2)}) %all-to-all-start.3) | async-done | bytes 2097184 | tf_op jit(solution)/shard_map/all_to_all | solution.py:26
  308.4 2.1 fusion
  310.5 3.6 %collective-permute-start = (bf16[512,128]{0,1:T(8,128)(2,1)S(1)}, bf16[512,128]{0,1:T(8,128)(2,1)S(1)}, u32[]{:S(2)}, u32[]{:S(2)}) collective-permute-start(bf16[512,128]{0,1:T(8,128)(2,1)S(1)} %fusion), channel_id=1, source_target_pairs={{0,8},{8,0},{1,9},{9,1},{2,10},{10,2},{3,11},{11,3},{4,12},{12,4},... | collective-permute-start | bytes 393224 | tf_op jit(solution)/shard_map/ppermute | solution.py:81
  314.2 0.5 subtract_convert_fusion
  314.7 2.1 subtract_convert_fusion.1
  316.8 2.1 subtract_convert_fusion.2
  318.9 2.1 subtract_convert_fusion.3
  321.0 1.0 copy.39
  (19 shorter events, 0.3 us)
Async XLA Ops:
  1.5 19.1 %all-to-all-start = ((bf16[64,32,1]{0,2,1:T(2,128)(2,1)}), bf16[64,32,1]{0,2,1:T(2,128)(2,1)S(1)}, u32[]{:S(2)}, u32[]{:S(2)}) async-start(bf16[64,32,1]{0,2,1:T(2,128)(2,1)} %copy.29), calls=%async_computation | async-start | bytes 32768 | tf_op jit(solution)/shard_map/all_to_all | solution.py:46
  20.5 22.5 %all-to-all-start.1 = ((bf16[64,32,128]{2,0,1:T(8,128)(2,1)}), bf16[64,32,128]{2,0,1:T(8,128)(2,1)S(1)}, u32[]{:S(2)}, u32[]{:S(2)}) async-start(bf16[64,32,128]{2,0,1:T(8,128)(2,1)} %copy.30), calls=%async_computation.1 | async-start | bytes 1048576 | tf_op jit(solution)/shard_map/all_to_all | solution.py:39
  43.7 0.8 copy-start.1
  44.5 7.2 %copy-start.3 = (bf16[2048,256]{1,0:T(8,128)(2,1)S(1)}, bf16[2048,256]{1,0:T(8,128)(2,1)}, u32[]{:S(2)}) copy-start(bf16[2048,256]{1,0:T(8,128)(2,1)} %param.7) | copy-start | bytes 3145732
  45.9 34.6 %all-to-all-start.2 = ((bf16[64,64,128]{2,1,0:T(8,128)(2,1)}), bf16[64,64,128]{2,1,0:T(8,128)(2,1)S(1)}, u32[]{:S(2)}, u32[]{:S(2)}) async-start(bf16[64,64,128]{2,1,0:T(8,128)(2,1)} %bitcast.8), calls=%async_computation.2 | async-start | bytes 2097152 | tf_op jit(solution)/shard_map/all_to_all | solution.py:69
  80.5 1.6 copy-start
  82.1 56.5 %all-to-all-start.6 = ((bf16[8,512,256]{1,2,0:T(8,128)(2,1)}), bf16[8,512,256]{1,2,0:T(8,128)(2,1)S(1)}, u32[]{:S(2)}, u32[]{:S(2)}) async-start(bf16[8,512,256]{1,2,0:T(8,128)(2,1)} %stack.11), calls=%async_computation.6 | async-start | bytes 4194304 | tf_op jit(solution)/shard_map/all_to_all | solution.py:26
  140.1 5.9 %copy-start.4 = (bf16[512,256]{1,0:T(8,128)(2,1)S(1)}, bf16[512,256]{1,0:T(8,128)(2,1)}, u32[]{:S(2)}) copy-start(bf16[512,256]{1,0:T(8,128)(2,1)} %get-tuple-element.6) | copy-start | bytes 786436
  140.1 55.9 %all-to-all-start.5 = ((bf16[8,512,256]{1,2,0:T(8,128)(2,1)}), bf16[8,512,256]{1,2,0:T(8,128)(2,1)}, u32[]{:S(2)}, u32[]{:S(2)}) async-start(bf16[8,512,256]{1,2,0:T(8,128)(2,1)} %stack.10), calls=%async_computation.5 | async-start | bytes 4194304 | tf_op jit(solution)/shard_map/all_to_all | solution.py:26
  197.6 53.2 %all-to-all-start.4 = ((bf16[8,512,256]{1,2,0:T(8,128)(2,1)}), bf16[8,512,256]{1,2,0:T(8,128)(2,1)}, u32[]{:S(2)}, u32[]{:S(2)}) async-start(bf16[8,512,256]{1,2,0:T(8,128)(2,1)} %stack.9), calls=%async_computation.4 | async-start | bytes 4194304 | tf_op jit(solution)/shard_map/all_to_all | solution.py:26
  252.3 56.1 %all-to-all-start.3 = ((bf16[8,512,256]{1,2,0:T(8,128)(2,1)}), bf16[8,512,256]{1,2,0:T(8,128)(2,1)}, u32[]{:S(2)}, u32[]{:S(2)}) async-start(bf16[8,512,256]{1,2,0:T(8,128)(2,1)} %stack.8), calls=%async_computation.3 | async-start | bytes 4194304 | tf_op jit(solution)/shard_map/all_to_all | solution.py:26
  260.4 53.7 %collective-permute-start.3 = (bf16[512,128]{0,1:T(8,128)(2,1)S(1)}, bf16[512,128]{0,1:T(8,128)(2,1)S(1)}, u32[]{:S(2)}, u32[]{:S(2)}) collective-permute-start(bf16[512,128]{0,1:T(8,128)(2,1)S(1)} %fusion.3), channel_id=1, source_target_pairs={{0,8},{8,0},{1,9},{9,1},{2,10},{10,2},{3,11},{11,3},{4,12},{12,4},... | collective-permute-start | bytes 393224 | tf_op jit(solution)/shard_map/ppermute | solution.py:81
  266.8 47.9 %collective-permute-start.2 = (bf16[512,128]{0,1:T(8,128)(2,1)}, bf16[512,128]{0,1:T(8,128)(2,1)}, u32[]{:S(2)}, u32[]{:S(2)}) collective-permute-start(bf16[512,128]{0,1:T(8,128)(2,1)} %fusion.2), channel_id=1, source_target_pairs={{0,8},{8,0},{1,9},{9,1},{2,10},{10,2},{3,11},{11,3},{4,12},{12,4},... | collective-permute-start | bytes 393224 | tf_op jit(solution)/shard_map/ppermute | solution.py:81
  273.3 43.5 %collective-permute-start.1 = (bf16[512,128]{0,1:T(8,128)(2,1)}, bf16[512,128]{0,1:T(8,128)(2,1)}, u32[]{:S(2)}, u32[]{:S(2)}) collective-permute-start(bf16[512,128]{0,1:T(8,128)(2,1)} %fusion.1), channel_id=1, source_target_pairs={{0,8},{8,0},{1,9},{9,1},{2,10},{10,2},{3,11},{11,3},{4,12},{12,4},... | collective-permute-start | bytes 393224 | tf_op jit(solution)/shard_map/ppermute | solution.py:81
  308.4 5.8 %copy-start.2 = (bf16[2048,128]{0,1:T(8,128)(2,1)S(1)}, bf16[2048,128]{0,1:T(8,128)(2,1)}, u32[]{:S(2)}) copy-start(bf16[2048,128]{0,1:T(8,128)(2,1)} %copy-done.1) | copy-start | bytes 1572868
  310.5 8.4 %collective-permute-start = (bf16[512,128]{0,1:T(8,128)(2,1)S(1)}, bf16[512,128]{0,1:T(8,128)(2,1)S(1)}, u32[]{:S(2)}, u32[]{:S(2)}) collective-permute-start(bf16[512,128]{0,1:T(8,128)(2,1)S(1)} %fusion), channel_id=1, source_target_pairs={{0,8},{8,0},{1,9},{9,1},{2,10},{10,2},{3,11},{11,3},{4,12},{12,4},... | collective-permute-start | bytes 393224 | tf_op jit(solution)/shard_map/ppermute | solution.py:81
